TPU v7x, 512 devices: a whole 4x4x16 slice. The times are simulated.
512 devices in a mesh: dp: 16 (over z_lo, core), center: 32 (over x, y, z_hi).
Axes of the slice: x: 4, y: 4, z: 16 (z_hi: 2, z_lo: 8; z = z_hi * 8 + z_lo), core: 2. Of those that a mesh axis runs over, the one named last changes fastest.
Arguments:
- features: bfloat16 [16384, 1024], P('dp'), may hold values from -6 to 6
- centers: bfloat16 [16384, 1024], P('center'), may hold values from -6 to 6
- targets: bfloat16 [16384, 256], P('dp'), may hold values from -6 to 6
Outputs:
- coef: float32 [16384, 256], P('center')
- residual: float32 [16384, 256], P('center')
All inputs are finite; a program needn't handle non-finite values.
Results may differ from a plain program's by a relative error of at most 0.024.
Values may be sent and summed in bfloat16 or wider, within the bound.
A program may use at most 64 MiB of HBM per device.

v0:
```python
import math

import jax
import jax.numpy as jnp
from jax import lax
from jax.sharding import PartitionSpec as P

BATCHES = 2
ITERS = 2


def in_blocks(array, dim, peers):
    shape = array.shape
    tiles = array.reshape(*shape[:dim], peers, shape[dim] // peers, *shape[dim + 1 :])
    return jnp.moveaxis(tiles, dim, 0)


def summed_on_arrival(array, axis, dim):
    peers = lax.axis_size(axis)
    tiles = lax.all_to_all(in_blocks(array, dim, peers), axis, 0, 0, tiled=True)
    return jnp.sum(tiles, axis=0)


def padded_to(lines, peers):
    spare = -len(lines) % peers
    return jnp.pad(lines, [(0, spare)] + [(0, 0)] * (lines.ndim - 1))


def joined_along(tiles, dim):
    shape = list(tiles.shape[1:])
    shape[dim] *= tiles.shape[0]
    return jnp.moveaxis(tiles, 0, dim).reshape(shape)


def from_everyone(array, axis):
    peers = lax.axis_size(axis)
    return lax.all_to_all(
        jnp.broadcast_to(array[None], (peers, *array.shape)), axis, 0, 0, tiled=True
    )


def collect(array, axis, dim):
    return joined_along(from_everyone(array, axis), dim)


def sum_by_parts(array, axes):
    lines = array.reshape(-1, array.shape[-1])
    own = summed_on_arrival(padded_to(lines, lax.axis_size(axes)), axes, 0)
    whole = collect(own, axes, 0)
    return whole[: len(lines)].reshape(array.shape)


def over_copies(array, axis):
    return from_everyone(array, axis).sum(axis=0)


def kernel_block(rows, centers):
    scores = lax.dot_general(
        rows, centers, (((1,), (1,)), ((), ())), preferred_element_type=jnp.float32
    )
    lifted = 1.0 + 0.5 / math.sqrt(rows.shape[1]) * scores
    return (lifted * lifted * lifted).astype(jnp.bfloat16)


def build_kernel(features, centers):
    batch_rows = features.shape[0] // BATCHES
    pieces = [
        kernel_block(features[batch_index * batch_rows : (batch_index + 1) * batch_rows], centers)
        for batch_index in range(BATCHES)
    ]
    return jnp.concatenate(pieces, axis=0)


def transposed_sum(kernel, values):
    local = lax.dot_general(
        kernel, values, (((0,), (0,)), ((), ())), preferred_element_type=jnp.float32
    )
    return sum_by_parts(local, "dp")


def column_sums(values):
    return over_copies(values, "center")


def whole_direction(direction):
    low_dir = direction.astype(jnp.bfloat16)
    return low_dir


def apply_operator(kernel, direction, total_rows):
    low_dir = whole_direction(direction)
    partial_value = jnp.dot(kernel, low_dir, preferred_element_type=jnp.float32)
    predicted = sum_by_parts(partial_value, "center").astype(jnp.bfloat16)
    return transposed_sum(kernel, predicted) / total_rows + 0.5 * direction


def on_device(features, centers, targets):
    total_rows = features.shape[0] * lax.axis_size("dp")
    kernel = build_kernel(features, centers)
    right_side = transposed_sum(kernel, targets) / math.sqrt(total_rows)
    coef = jnp.zeros_like(right_side)
    residual = right_side
    direction = right_side
    norm_now = column_sums(jnp.sum(residual * residual, axis=0))
    for turn in range(ITERS):
        image = apply_operator(kernel, direction, total_rows)
        curvature = column_sums(jnp.sum(direction * image, axis=0))
        step_size = norm_now / (curvature + 1e-06)
        coef = coef + step_size * direction
        residual = residual - step_size * image
        if turn + 1 < ITERS:
            norm_next = column_sums(jnp.sum(residual * residual, axis=0))
            direction = residual + norm_next / (norm_now + 1e-06) * direction
            norm_now = norm_next
    return (coef, residual)


def solution(mesh):
    placed = (P("dp", None), P("center", None), P("dp", None))
    return jax.shard_map(
        on_device,
        mesh=mesh,
        in_specs=placed,
        out_specs=(P("center", None), P("center", None)),
        check_vma=False,
    )
```

profile of v0, /device:TPU:1, one launch (start us, length us, event | category | flops | bytes accessed | tf_op | source)
XLA Modules:
  0.0 494.5 jit_solution(3436608047167978663)
XLA Ops:
  0.6 0.0 copy-start
  0.6 0.0 copy-start.3
  0.7 1.2 copy-done
  1.9 2.0 fusion.3
  3.9 0.0 copy-done.3
  3.9 0.0 copy-start.4
  3.9 0.8 fusion.2
  4.6 0.3 copy-done.4
  4.9 0.0 copy-start.2
  4.9 0.5 fusion.15
  5.4 0.3 copy-done.2
  5.7 40.0 %all_to_all.74 = f32[16,32,256]{2,1,0:T(8,128)S(1)} all-to-all(f32[16,32,256]{2,1,0:T(8,128)S(1)} %bitcast.73), channel_id=1, replica_groups=mesh['dp'=16,'center'=32] {'dp'}, dimensions={0} | all-to-all | bytes 1048576 | tf_op jit(solution)/shard_map/all_to_all | solution.py:20
  45.8 0.8 broadcast_in_dim.18
  46.6 7.1 %all-to-all-start.1 = ((f32[16,32,256]{2,1,0:T(8,128)}), f32[16,32,256]{2,1,0:T(8,128)S(1)}, u32[]{:S(2)}, u32[]{:S(2)}) async-start(f32[16,32,256]{2,1,0:T(8,128)} %broadcast_in_dim.18), calls=%async_computation.1 | async-start | bytes 1048576 | tf_op jit(solution)/shard_map/all_to_all | solution.py:37
  53.7 2.2 pad_maximum_fusion
  55.9 24.1 %all-to-all-done.1 = f32[16,32,256]{2,1,0:T(8,128)S(1)} async-done(((f32[16,32,256]{2,1,0:T(8,128)}), f32[16,32,256]{2,1,0:T(8,128)S(1)}, u32[]{:S(2)}, u32[]{:S(2)}) %all-to-all-start.1) | async-done | bytes 524320 | tf_op jit(solution)/shard_map/all_to_all | solution.py:37
  80.0 0.4 fusion.16
  80.4 43.9 %all_to_all.75 = f32[32,32,256]{2,1,0:T(8,128)} all-to-all(f32[32,32,256]{2,1,0:T(8,128)S(1)} %fusion.16), channel_id=1, replica_groups=mesh['dp'=16,'center'=32] {'center'}, dimensions={0} | all-to-all | bytes 2097152 | tf_op jit(solution)/shard_map/all_to_all | solution.py:20
  124.3 1.3 reduce_sum.120
  125.6 0.9 broadcast_in_dim.20
  126.4 3.9 all-to-all-start.4
  130.3 2.3 copy.10
  132.6 23.4 %all-to-all-done.4 = bf16[32,32,256]{2,1,0:T(8,128)(2,1)S(1)} async-done(((bf16[32,32,256]{2,1,0:T(8,128)(2,1)}), bf16[32,32,256]{2,1,0:T(8,128)(2,1)S(1)}, u32[]{:S(2)}, u32[]{:S(2)}) %all-to-all-start.4) | async-done | bytes 524320 | tf_op jit(solution)/shard_map/all_to_all | solution.py:37
  156.0 1.7 fusion.17
  157.7 61.7 %all_to_all.76 = f32[16,32,256]{2,1,0:T(8,128)S(1)} all-to-all(f32[16,32,256]{2,1,0:T(8,128)S(1)} %fusion.17), channel_id=1, replica_groups=mesh['dp'=16,'center'=32] {'dp'}, dimensions={0} | all-to-all | bytes 1048576 | tf_op jit(solution)/shard_map/all_to_all | solution.py:20
  219.5 33.1 %all_to_all.77 = f32[16,32,256]{2,1,0:T(8,128)S(1)} all-to-all(f32[16,32,256]{2,1,0:T(8,128)S(1)} %broadcast_in_dim.21), channel_id=1, replica_groups=mesh['dp'=16,'center'=32] {'dp'}, dimensions={0} | all-to-all | bytes 1048576 | tf_op jit(solution)/shard_map/all_to_all | solution.py:37
  252.5 0.2 multiply_reduce_fusion.2
  252.7 19.1 %all_to_all.78 = f32[32,1,256]{2,1,0:T(1,128)S(1)} all-to-all(f32[32,1,256]{2,1,0:T(1,128)S(1)} %broadcast_in_dim.22), channel_id=1, replica_groups=mesh['dp'=16,'center'=32] {'center'}, dimensions={0} | all-to-all | bytes 65536 | tf_op jit(solution)/shard_map/all_to_all | solution.py:37
  271.8 0.6 broadcast_in_dim.19
  272.5 3.9 all-to-all-start.2
  276.3 0.1 reduce_sum.123
  276.4 15.8 %all-to-all-done.2 = f32[32,1,256]{2,1,0:T(1,128)S(1)} async-done(((f32[32,1,256]{2,1,0:T(1,128)}), f32[32,1,256]{2,1,0:T(1,128)S(1)}, u32[]{:S(2)}, u32[]{:S(2)}) %all-to-all-start.2) | async-done | bytes 32800 | tf_op jit(solution)/shard_map/all_to_all | solution.py:37
  292.2 0.1 reduce_sum.119
  292.2 0.2 multiply_reduce_fusion.1
  292.4 19.3 %all_to_all.79 = f32[32,1,256]{2,1,0:T(1,128)S(1)} all-to-all(f32[32,1,256]{2,1,0:T(1,128)S(1)} %broadcast_in_dim.23), channel_id=1, replica_groups=mesh['dp'=16,'center'=32] {'center'}, dimensions={0} | all-to-all | bytes 65536 | tf_op jit(solution)/shard_map/all_to_all | solution.py:37
  311.7 0.1 reduce_sum.125
  311.8 0.2 fusion.12
  312.0 0.4 fusion.18
  312.4 0.0 copy-start.1
  312.4 32.1 %all_to_all.80 = f32[32,32,256]{2,1,0:T(8,128)} all-to-all(f32[32,32,256]{2,1,0:T(8,128)S(1)} %fusion.18), channel_id=1, replica_groups=mesh['dp'=16,'center'=32] {'center'}, dimensions={0} | all-to-all | bytes 2097152 | tf_op jit(solution)/shard_map/all_to_all | solution.py:20
  344.5 1.3 reduce_sum.126
  345.8 0.1 broadcast_in_dim.24
  345.9 33.0 %all_to_all.81 = bf16[32,32,256]{2,1,0:T(8,128)(2,1)S(1)} all-to-all(bf16[32,32,256]{2,1,0:T(8,128)(2,1)S(1)} %broadcast_in_dim.24), channel_id=1, replica_groups=mesh['dp'=16,'center'=32] {'center'}, dimensions={0} | all-to-all | bytes 1048576 | tf_op jit(solution)/shard_map/all_to_all | solution.py:37
  378.9 0.0 copy-done.1
  378.9 0.5 fusion.19
  379.3 57.8 %all_to_all.82 = f32[16,32,256]{2,1,0:T(8,128)S(1)} all-to-all(f32[16,32,256]{2,1,0:T(8,128)S(1)} %fusion.19), channel_id=1, replica_groups=mesh['dp'=16,'center'=32] {'dp'}, dimensions={0} | all-to-all | bytes 1048576 | tf_op jit(solution)/shard_map/all_to_all | solution.py:20
  437.2 33.1 %all_to_all.83 = f32[16,32,256]{2,1,0:T(8,128)S(1)} all-to-all(f32[16,32,256]{2,1,0:T(8,128)S(1)} %broadcast_in_dim.25), channel_id=1, replica_groups=mesh['dp'=16,'center'=32] {'dp'}, dimensions={0} | all-to-all | bytes 1048576 | tf_op jit(solution)/shard_map/all_to_all | solution.py:37
  470.3 0.3 broadcast_multiply_fusion
  470.6 22.6 %all_to_all.84 = f32[32,1,256]{2,1,0:T(1,128)S(1)} all-to-all(f32[32,1,256]{2,1,0:T(1,128)S(1)} %broadcast_in_dim.26), channel_id=1, replica_groups=mesh['dp'=16,'center'=32] {'center'}, dimensions={0} | all-to-all | bytes 65536 | tf_op jit(solution)/shard_map/all_to_all | solution.py:37
  493.2 0.1 reduce_sum.129
  493.3 1.2 fusion.7
  (12 shorter events, 0.3 us)
Async XLA Ops:
  0.6 1.2 copy-start
  0.6 3.2 copy-start.3
  3.9 1.0 copy-start.4
  4.9 0.8 copy-start.2
  46.6 33.3 %all-to-all-start.1 = ((f32[16,32,256]{2,1,0:T(8,128)}), f32[16,32,256]{2,1,0:T(8,128)S(1)}, u32[]{:S(2)}, u32[]{:S(2)}) async-start(f32[16,32,256]{2,1,0:T(8,128)} %broadcast_in_dim.18), calls=%async_computation.1 | async-start | bytes 1048576 | tf_op jit(solution)/shard_map/all_to_all | solution.py:37
  126.4 29.6 %all-to-all-start.4 = ((bf16[32,32,256]{2,1,0:T(8,128)(2,1)}), bf16[32,32,256]{2,1,0:T(8,128)(2,1)S(1)}, u32[]{:S(2)}, u32[]{:S(2)}) async-start(bf16[32,32,256]{2,1,0:T(8,128)(2,1)} %broadcast_in_dim.20), calls=%async_computation.4 | async-start | bytes 1048576 | tf_op jit(solution)/shard_map/all_to_all | solution.py:37
  272.5 19.7 %all-to-all-start.2 = ((f32[32,1,256]{2,1,0:T(1,128)}), f32[32,1,256]{2,1,0:T(1,128)S(1)}, u32[]{:S(2)}, u32[]{:S(2)}) async-start(f32[32,1,256]{2,1,0:T(1,128)} %broadcast_in_dim.19), calls=%async_computation.2 | async-start | bytes 65536 | tf_op jit(solution)/shard_map/all_to_all | solution.py:37
  312.4 66.5 %copy-start.1 = (bf16[512,1024]{1,0:T(8,128)(2,1)S(1)}, bf16[512,1024]{1,0:T(8,128)(2,1)}, u32[]{:S(2)}) copy-start(bf16[512,1024]{1,0:T(8,128)(2,1)} %copy.10) | copy-start | bytes 3145732
where the time goes:
time: 496 us; the launch traced here: 495 us
  blocking collectives  396 us (80%)
  waiting for transfers between devices  63.2 us (13%)
  starting transfers between devices  14.8 us (3%)
  other arithmetic  7.1 us (1%)
  local copies, waits for them, and re-layouts  6.63 us (1%)
  matrix products  6.19 us (1%)
    all_to_all x5, blocking collectives, summed_on_arrival(): tiles = lax.all_to_all(in_blocks(array, dim, peers), axis, 0, 0, tiled=True)  236 us
    all_to_all x6, blocking collectives, from_everyone(): lax.all_to_all(jnp.broadcast_to(array[None], (peers, *array.shape)), axis...  160 us
    all_to_all x3, waiting for transfers between devices, from_everyone(): lax.all_to_all(jnp.broadcast_to(array[None], (peers, *array.shape)), axis...  63.2 us
    all_to_all x3, starting transfers between devices, from_everyone(): lax.all_to_all(jnp.broadcast_to(array[None], (peers, *array.shape)), axis...  14.8 us
  transfers between devices with their start and end apart: 3, of which 3 were waited for; matrix products, arithmetic and copies ran while one was open for 1% of the time, Pallas kernels for 0%

commit v1 on v0

v1 whole, which is shorter than its diff:
```python
import functools
import math

import jax
import jax.numpy as jnp
from jax import lax
from jax.experimental import pallas as pl
from jax.experimental.pallas import tpu as pltpu
from jax.sharding import PartitionSpec as P

MESH = pl.DeviceIdType.MESH
F32, BF16 = jnp.float32, jnp.bfloat16
EPS = 1e-06


def nt(a, b):
    return lax.dot_general(a, b, (((1,), (1,)), ((), ())), preferred_element_type=F32)


def nn(a, b):
    return lax.dot_general(a, b, (((1,), (0,)), ((), ())), preferred_element_type=F32)


def total(x):
    return jnp.sum(x, axis=1, keepdims=True)


def diagonal(slot):
    lane = lax.broadcasted_iota(jnp.int32, (16, 128), 1)
    return lane == lax.broadcasted_iota(jnp.int32, (16, 128), 0) + 16 * slot


def to_row(*columns):
    held = jnp.zeros((16, 128), F32)
    for slot, column in enumerate(columns):
        held = jnp.where(diagonal(slot), column, held)
    return jnp.sum(held, axis=0, keepdims=True)


def from_row(row, slot):
    return total(jnp.where(diagonal(slot), jnp.broadcast_to(row, (16, 128)), 0.0))


def copy_to(src, dst, send, recv, where):
    return pltpu.make_async_remote_copy(
        src_ref=src, dst_ref=dst, send_sem=send, recv_sem=recv, device_id=where, device_id_type=MESH
    )


def loop(count, body):
    def step(k, carry):
        body(k)
        return carry

    lax.fori_loop(0, count, step, 0)


def kernel(
    n_total, f_ref, c_ref, t_ref, coef_ref, res_ref,
    kern, tt, part, chip, pair_in, his, hir, los, lor, bg, dg, rg,
    ps, pr, hs, hr, ph, sts, str_, wr, rems, remr, sns, snr, fins, finr, bacc, dacc, racc,
    pair_s, pair_r, hi_s, hi_r, lo_s, lo_r, ag_s, ag_r, sib_s, sib_r,
    xs_s, xs_r, cr_s, cr_r, xg_s, xg_r, st_s, st_r, w_s, w_r, rem_s, rem_r, sn_s, sn_r, fin_s, fin_r,
):
    g, j = lax.axis_index("dp"), lax.axis_index("center")
    zl, c = lax.div(g, 2), lax.rem(g, 2)
    xy, zh = lax.div(j, 2), lax.rem(j, 2)
    o = c * 8 + zl
    sibling = (zl * 2 + (1 - c), j)
    across = (g, xy * 2 + (1 - zh))

    def line(z):
        return (z * 2 + c, j)

    def any_dp(p):
        return (lax.rem(p, 8) * 2 + lax.div(p, 8), j)

    def plane(p):
        return (g, p * 2 + zh)

    def any_center(p):
        return (g, p)

    barrier = pltpu.get_barrier_semaphore()

    def greet_dp(k):
        pl.semaphore_signal(barrier, inc=1, device_id=any_dp(lax.rem(o + k + 1, 16)), device_id_type=MESH)

    def greet_center(k):
        pl.semaphore_signal(barrier, inc=1, device_id=any_center(lax.rem(j + k + 1, 32)), device_id_type=MESH)

    loop(15, greet_dp)
    loop(31, greet_center)

    scale = 0.5 / math.sqrt(f_ref.shape[1])

    def kernel_tile(k):
        rows = pl.ds(pl.multiple_of(lax.div(k, 2) * 256, 256), 256)
        cols = pl.ds(pl.multiple_of(lax.rem(k, 2) * 256, 256), 256)
        lifted = 1.0 + scale * nt(f_ref[rows, :], c_ref[cols, :])
        kern[rows, cols] = (lifted * lifted * lifted).astype(BF16)

    loop(8, kernel_tile)

    def turn_targets(k):
        at = pl.ds(pl.multiple_of(k * 256, 256), 256)
        tt[:, at] = jnp.transpose(t_ref[at, :].astype(F32)).astype(BF16)

    loop(4, turn_targets)

    def weigh(k, held):
        rows = pl.ds(pl.multiple_of(k * 64, 64), 64)
        return held + jnp.sum(kern[rows, :].astype(F32), axis=0, keepdims=True)

    wr[o] = lax.fori_loop(0, 16, weigh, jnp.zeros((1, 512), F32))

    def project(values):
        def tile(k):
            cols = pl.ds(pl.multiple_of(k * 256, 256), 256)
            part[:, :, cols] = nn(values(), kern[:, cols]).reshape(16, 16, 256)

        loop(2, tile)

    def pair_up(step):
        copy = copy_to(
            part.at[pl.ds((1 - c) * 8, 8)], pair_in.at[step], pair_s.at[step], pair_r.at[step], sibling
        )
        copy.start()
        return copy

    def pairs(copy, step):
        copy.wait()

        def add(z):
            chip[z] = part[c * 8 + z] + pair_in[step, z]

        loop(8, add)

    def along_line(src, dst, send, recv):
        def go(k):
            z = lax.rem(zl + k + 1, 8)
            copy_to(src.at[z], dst.at[zl], send.at[z], recv.at[zl], line(z)).start()

        loop(7, go)

    def line_arrived(src, dst, send, recv):
        def take(k):
            z = lax.rem(zl + k + 1, 8)
            copy_to(src.at[z], dst.at[z], send.at[z], recv.at[z], line(z)).wait()

        loop(7, take)

    def line_sum(src, dst):
        def add(k, held):
            return held + dst[lax.rem(zl + k + 1, 8)].astype(F32)

        return lax.fori_loop(0, 7, add, src[zl].astype(F32))

    def share_columns(buf, step):
        mine = buf.at[o]

        def go(k):
            z = lax.rem(zl + k + 1, 8)
            copy_to(mine, mine, ag_s.at[step, z], ag_r.at[step, zl], line(z)).start()

        loop(7, go)
        copy_to(mine, mine, sib_s.at[step, zl], sib_r.at[step, zl], sibling).start()

        def relay(k):
            z = lax.rem(zl + k + 1, 8)
            piece = buf.at[c * 8 + z]
            copy_to(piece, piece, ag_s.at[step, z], ag_r.at[step, z], line(z)).wait_recv()
            copy_to(piece, piece, sib_s.at[step, z], sib_r.at[step, z], sibling).start()

        loop(7, relay)

        def from_sibling(z):
            piece = buf.at[(1 - c) * 8 + z]
            copy_to(piece, piece, sib_s.at[step, z], sib_r.at[step, z], sibling).wait()

        loop(8, from_sibling)

        def sent(k):
            z = lax.rem(zl + k + 1, 8)
            copy_to(mine, mine, ag_s.at[step, z], ag_r.at[step, z], line(z)).wait_send()

        loop(7, sent)

    def broadcast(src, dst, me, count, send, recv, where):
        def go(k):
            p = lax.rem(me + k + 1, count)
            copy_to(src, dst.at[me], send.at[p], recv.at[me], where(p)).start()

        loop(count - 1, go)

    def scatter(src, dst, me, count, send, recv, where):
        def go(k):
            p = lax.rem(me + k + 1, count)
            copy_to(src.at[p], dst.at[me], send.at[p], recv.at[me], where(p)).start()

        loop(count - 1, go)

    def gathered(dst, me, count, send, recv, where):
        def take(k):
            p = lax.rem(me + k + 1, count)
            copy_to(dst.at[p], dst.at[p], send.at[p], recv.at[p], where(p)).wait()

        loop(count - 1, take)

    def predict(buf, step):
        def tile(k):
            cols = pl.ds(pl.multiple_of(k * 256, 256), 256)
            values = buf[...].reshape(256, 512)
            ps[step, :, :, cols] = nt(values, kern[cols, :]).astype(BF16).reshape(16, 16, 256)

        loop(4, tile)
        scatter(ps.at[step], pr.at[step], xy, 16, xs_s.at[step], xs_r.at[step], plane)
        gathered(pr.at[step], xy, 16, xs_s.at[step], xs_r.at[step], plane)

        def add(k, held):
            return held + pr[step, lax.rem(xy + k + 1, 16)].astype(F32)

        hs[step] = lax.fori_loop(0, 15, add, ps[step, xy].astype(F32)).astype(BF16)
        cross = copy_to(hs.at[step], hr.at[step], cr_s.at[step], cr_r.at[step], across)
        cross.start()
        cross.wait()
        ph[step, xy] = (hs[step].astype(F32) + hr[step].astype(F32)).astype(BF16)
        broadcast(ph.at[step, xy], ph.at[step], xy, 16, xg_s.at[step], xg_r.at[step], plane)
        gathered(ph.at[step], xy, 16, xg_s.at[step], xg_r.at[step], plane)

    def image_of(step):
        project(lambda: ph[step].reshape(256, 1024))

        def deflate(p):
            block = ph[step, p].astype(F32)
            middle = total(block) * (1.0 / block.shape[1])
            sts[step, p] = to_row(total(block * block), middle)
            part[p] = part[p] - middle * wr[o]

        loop(16, deflate)
        copy = pair_up(1 + step)
        str_[step, o] = sts[step, o]
        scatter(sts.at[step], str_.at[step], o, 16, st_s.at[step], st_r.at[step], any_dp)
        pairs(copy, 1 + step)

        def narrow(z):
            rems[step, z] = chip[z].astype(BF16)

        loop(8, narrow)
        along_line(rems.at[step], remr.at[step], rem_s.at[step], rem_r.at[step])
        gathered(str_.at[step], o, 16, st_s.at[step], st_r.at[step], any_dp)

        def add(p, held):
            return held + str_[step, p]

        squares = from_row(lax.fori_loop(0, 16, add, jnp.zeros((1, 128), F32)), 0)

        def lift(p, held):
            return held + from_row(str_[step, p], 1) * wr[p]

        lifted = lax.fori_loop(0, 16, lift, jnp.zeros((16, 512), F32))
        line_arrived(rems.at[step], remr.at[step], rem_s.at[step], rem_r.at[step])
        return line_sum(rems.at[step], remr.at[step]) + lifted, squares

    def center_start(step, *columns):
        snr[step, j] = to_row(*columns)
        broadcast(snr.at[step, j], snr.at[step], j, 32, sn_s.at[step], sn_r.at[step], any_center)

    def center_sum(step):
        gathered(snr.at[step], j, 32, sn_s.at[step], sn_r.at[step], any_center)
        return jnp.sum(snr[step].reshape(32, 128), axis=0, keepdims=True)

    project(lambda: tt[...])
    pl.semaphore_wait(barrier, 46)
    copy = pair_up(0)
    broadcast(wr.at[o], wr, o, 16, w_s, w_r, any_dp)
    pairs(copy, 0)

    def split(z):
        high = chip[z].astype(BF16)
        his[z] = high
        los[z] = (chip[z] - high.astype(F32)).astype(BF16)

    loop(8, split)
    along_line(his, hir, hi_s, hi_r)
    line_arrived(his, hir, hi_s, hi_r)
    unscale = 1.0 / math.sqrt(n_total)
    bacc[...] = line_sum(his, hir)
    bg[o] = (bacc[...] * unscale).astype(BF16)
    share_columns(bg, 0)
    along_line(los, lor, lo_s, lo_r)
    predict(bg, 0)

    line_arrived(los, lor, lo_s, lo_r)
    bacc[...] = (bacc[...] + line_sum(los, lor)) * unscale
    center_start(0, total(bacc[...] * bacc[...]))
    gathered(wr, o, 16, w_s, w_r, any_dp)
    summed, squares = image_of(0)
    norm = from_row(center_sum(0), 0)
    image = summed * (1.0 / n_total) + 0.5 * bacc[...]
    guess = norm / (squares * (1.0 / n_total) + 0.5 * norm + EPS)
    near = bacc[...] - guess * image
    center_start(1, total(bacc[...] * image), total(near * near), total(near * image), total(image * image))
    dacc[...] = image
    sums = center_sum(1)
    step_0 = norm / (from_row(sums, 0) + EPS)
    off = step_0 - guess
    norm_1 = from_row(sums, 1) - 2.0 * off * from_row(sums, 2) + off * off * from_row(sums, 3)
    racc[...] = bacc[...] - step_0 * dacc[...]
    dacc[...] = racc[...] + norm_1 / (norm + EPS) * bacc[...]
    dg[o] = dacc[...].astype(BF16)
    share_columns(dg, 1)
    center_start(2, total(dacc[...] * dacc[...]))
    predict(dg, 1)

    summed, squares = image_of(1)
    image = summed * (1.0 / n_total) + 0.5 * dacc[...]
    curvature = squares * (1.0 / n_total) + 0.5 * from_row(center_sum(2), 0)
    step_1 = norm_1 / (curvature + EPS)
    rg[o] = (racc[...] - step_1 * image).astype(BF16)
    finr[o] = to_row(step_0, step_1)
    broadcast(finr.at[o], finr, o, 16, fin_s, fin_r, any_dp)
    share_columns(rg, 2)
    gathered(finr, o, 16, fin_s, fin_r, any_dp)

    def finish(p):
        first, second = from_row(finr[p], 0), from_row(finr[p], 1)
        part[p] = first * bg[p].astype(F32) + second * dg[p].astype(F32)

    loop(16, finish)

    def turn(k):
        rows = pl.ds(pl.multiple_of(k * 128, 128), 128)
        coef_ref[rows, :] = jnp.transpose(part[:, :, rows].reshape(256, 128))
        res_ref[rows, :] = jnp.transpose(rg[:, :, rows].astype(F32).reshape(256, 128))

    loop(4, turn)


def on_device(features, centers, targets):
    n_total = features.shape[0] * lax.axis_size("dp")
    vmem, dma = pltpu.VMEM, pltpu.SemaphoreType.DMA
    whole = pl.BlockSpec(memory_space=pltpu.VMEM)
    out = jax.ShapeDtypeStruct((centers.shape[0], targets.shape[1]), F32)
    buffers = [
        vmem((1024, 512), BF16), vmem((256, 1024), BF16), vmem((16, 16, 512), F32), vmem((8, 16, 512), F32),
        vmem((3, 8, 16, 512), F32), vmem((8, 16, 512), BF16), vmem((8, 16, 512), BF16),
        vmem((8, 16, 512), BF16), vmem((8, 16, 512), BF16),
        vmem((16, 16, 512), BF16), vmem((16, 16, 512), BF16), vmem((16, 16, 512), BF16),
        vmem((2, 16, 16, 1024), BF16), vmem((2, 16, 16, 1024), BF16),
        vmem((2, 16, 1024), BF16), vmem((2, 16, 1024), BF16), vmem((2, 16, 16, 1024), BF16),
        vmem((2, 16, 1, 128), F32), vmem((2, 16, 1, 128), F32), vmem((16, 1, 512), F32),
        vmem((2, 8, 16, 512), BF16), vmem((2, 8, 16, 512), BF16),
        vmem((1, 1, 128), F32), vmem((3, 32, 1, 128), F32), vmem((1, 1, 128), F32), vmem((16, 1, 128), F32),
        vmem((16, 512), F32), vmem((16, 512), F32), vmem((16, 512), F32),
    ]
    semaphores = []
    for shape in ((3,), (8,), (8,), (3, 8), (3, 8), (2, 16), (2,), (2, 16), (2, 16), (16,), (2, 8), (3, 32), (16,)):
        semaphores += [dma(shape), dma(shape)]
    return pl.pallas_call(
        functools.partial(kernel, n_total),
        out_shape=(out, out),
        in_specs=[whole] * 3,
        out_specs=(whole, whole),
        scratch_shapes=buffers + semaphores,
        compiler_params=pltpu.CompilerParams(
            collective_id=0, has_side_effects=True, vmem_limit_bytes=40 * 1024 * 1024
        ),
    )(features, centers, targets)


def solution(mesh):
    placed = (P("dp", None), P("center", None), P("dp", None))
    return jax.shard_map(
        on_device,
        mesh=mesh,
        in_specs=placed,
        out_specs=(P("center", None), P("center", None)),
        check_vma=False,
    )
```

time: 496 us -> 157 us (0.32)
  blocking collectives: 396 us -> 0 us
  Pallas kernels: 0 us -> 151 us
  waiting for transfers between devices: 63.2 us -> 0 us
  starting transfers between devices: 14.8 us -> 0 us
  other arithmetic: 7.1 us -> 0 us
  matrix products: 6.19 us -> 0 us
    all_to_all x11 -> x0, blocking collectives: 396 us -> none  [the longest x5 236 us: summed_on_arrival(): tiles = lax.all_to_all(in_blocks(array, dim, peers), axis, 0, 0, tiled=True)]
    pallas_call x0 -> x1, Pallas kernels: none -> 151 us  [on_device(): pl.pallas_call(functools.partial(kernel, n_total), out_shape=(out, out),...]
    all_to_all x3 -> x0, waiting for transfers between devices: 63.2 us -> none  [from_everyone(): lax.all_to_all(jnp.broadcast_to(array[None], (peers, *array.shape)), axis...]
    all_to_all x3 -> x0, starting transfers between devices: 14.8 us -> none  [from_everyone(): lax.all_to_all(jnp.broadcast_to(array[None], (peers, *array.shape)), axis...]
    dot_general x7 -> x0, matrix products: 6.19 us -> none  [the longest x2 2.75 us: kernel_block(): lax.dot_general(rows, centers, (((1,), (1,)), ((), ())), preferred_elemen...]
  transfers between devices with their start and end apart: 3 -> 0, of which waited for: 3 -> 0; matrix products, arithmetic and copies ran while one was open for 1% -> 0% of each run, Pallas kernels for 0% -> 0%
where the time goes in v1:
time: 157 us
  Pallas kernels  151 us (96%)
  local copies, waits for them, and re-layouts  5.44 us (3%)
    pallas_call x1, Pallas kernels, on_device(): pl.pallas_call(functools.partial(kernel, n_total), out_shape=(out, out),...  151 us
    unnamed x8, local copies, waits for them, and re-layouts  5.44 us

profile of v1, /device:TPU:1, one launch (start us, length us, event | category | flops | bytes accessed | tf_op | source)
XLA Modules:
  0.0 156.9 jit_solution(16334536827125588463)
XLA Ops:
  0.6 0.0 copy-start
  0.6 1.6 %copy-done = bf16[1024,1024]{1,0:T(8,128)(2,1)S(1)} copy-done((bf16[1024,1024]{1,0:T(8,128)(2,1)S(1)}, bf16[1024,1024]{1,0:T(8,128)(2,1)}, u32[]{:S(2)}) %copy-start) | copy-done | bytes 2097176
  2.2 0.0 copy-start.1
  2.2 1.2 copy-done.1
  3.4 0.0 copy-start.2
  3.4 1.0 copy-done.2
  4.5 150.8 %shard_map.50 = (f32[512,256]{1,0:T(8,128)S(1)}, f32[512,256]{1,0:T(8,128)S(1)}) custom-call(bf16[1024,1024]{1,0:T(8,128)(2,1)S(1)} %copy-done, bf16[512,1024]{1,0:T(8,128)(2,1)S(1)} %copy-done.1, bf16[1024,256]{1,0:T(8,128)(2,1)S(1)} %copy-done.2), custom_call_target="tpu_custom_call" | custom-call | tf_op jit(solution)/shard_map/pallas_call | solution.py:360
  155.3 0.8 copy.7
  156.1 0.8 copy.8
Async XLA Ops:
  0.6 1.6 %copy-start = (bf16[1024,1024]{1,0:T(8,128)(2,1)S(1)}, bf16[1024,1024]{1,0:T(8,128)(2,1)}, u32[]{:S(2)}) copy-start(bf16[1024,1024]{1,0:T(8,128)(2,1)} %f_ref.1) | copy-start | bytes 6291460
  2.2 1.2 copy-start.1
  3.4 1.0 copy-start.2

commit v2 on v1

v2 whole, which is shorter than its diff:
```python
import functools
import math

import jax
import jax.numpy as jnp
from jax import lax
from jax.experimental import pallas as pl
from jax.experimental.pallas import tpu as pltpu
from jax.sharding import PartitionSpec as P

MESH = pl.DeviceIdType.MESH
F32, BF16 = jnp.float32, jnp.bfloat16
EPS = 1e-06


def nt(a, b):
    return lax.dot_general(a, b, (((1,), (1,)), ((), ())), preferred_element_type=F32)


def nn(a, b):
    return lax.dot_general(a, b, (((1,), (0,)), ((), ())), preferred_element_type=F32)


def total(x):
    return jnp.sum(x, axis=1, keepdims=True)


def diagonal(slot):
    lane = lax.broadcasted_iota(jnp.int32, (8, 128), 1)
    return lane == lax.broadcasted_iota(jnp.int32, (8, 128), 0) + 16 * slot


def to_row(*columns):
    held = jnp.zeros((8, 128), F32)
    for slot, column in enumerate(columns):
        held = jnp.where(diagonal(slot), column, held)
    return jnp.sum(held, axis=0, keepdims=True)


def from_row(row, slot):
    return total(jnp.where(diagonal(slot), jnp.broadcast_to(row, (8, 128)), 0.0))


def copy_to(src, dst, send, recv, where):
    return pltpu.make_async_remote_copy(
        src_ref=src, dst_ref=dst, send_sem=send, recv_sem=recv, device_id=where, device_id_type=MESH
    )


def loop(count, body):
    def step(k, carry):
        body(k)
        return carry

    lax.fori_loop(0, count, step, 0)


def kernel(
    n_total, f_hbm, c_hbm, t_hbm, coef_ref, res_ref,
    f_ref, c_ref, t_ref, kern, tt, part, chip, pair_in, his, hir, los, lor, vec,
    ps, pr, hs, hr, ph, sts, str_, wr, rems, remr, snr, scn, finr, bacc, dacc, racc,
    load_f, load_c, load_t,
    pair_s, pair_r, hi_s, hi_r, lo_s, lo_r, ag_s, ag_r, sib_s, sib_r,
    xs_s, xs_r, cr_s, cr_r, xg_s, xg_r, st_s, st_r, w_s, w_r, rem_s, rem_r, sn_s, sn_r, sc_s, sc_r, fin_s, fin_r,
):
    g, j = lax.axis_index("dp"), lax.axis_index("center")
    zl, c = lax.div(g, 2), lax.rem(g, 2)
    xy, zh = lax.div(j, 2), lax.rem(j, 2)
    o = c * 8 + zl
    sibling = (zl * 2 + (1 - c), j)
    across = (g, xy * 2 + (1 - zh))

    def line(z):
        return (z * 2 + c, j)

    def any_dp(p):
        return (lax.rem(p, 8) * 2 + lax.div(p, 8), j)

    def plane(p):
        return (g, p * 2 + zh)

    barrier = pltpu.get_barrier_semaphore()

    def greet(where):
        pl.semaphore_signal(barrier, inc=1, device_id=where, device_id_type=MESH)

    greet(across)
    loop(15, lambda k: greet(any_dp(lax.rem(o + k + 1, 16))))
    loop(15, lambda k: greet(plane(lax.rem(xy + k + 1, 16))))

    scale = 0.5 / math.sqrt(f_ref.shape[1])
    unscale = 1.0 / math.sqrt(n_total)
    quarter = f_ref.shape[0] // 4

    def rows_at(k, size):
        return pl.ds(pl.multiple_of(k * size, size), size)

    def load(k):
        return pltpu.make_async_copy(f_hbm.at[rows_at(k, quarter)], f_ref.at[rows_at(k, quarter)], load_f.at[k])

    centers_in = pltpu.make_async_copy(c_hbm, c_ref, load_c)
    targets_in = pltpu.make_async_copy(t_hbm, t_ref, load_t)
    centers_in.start()
    loop(4, lambda k: load(k).start())
    targets_in.start()
    centers_in.wait()

    def kernel_rows(k):
        load(k).wait()
        rows = rows_at(k, quarter)

        def tile(i):
            cols = rows_at(i, 256)
            lifted = 1.0 + scale * nt(f_ref[rows, :], c_ref[cols, :])
            kern[rows, cols] = (lifted * lifted * lifted).astype(BF16)

        loop(2, tile)

    loop(4, kernel_rows)
    targets_in.wait()

    def turn_targets(k):
        at = rows_at(k, 256)
        turned = jnp.transpose(t_ref[at, :].astype(F32)).astype(BF16)
        tt[0, :, at] = turned[:128]
        tt[1, :, at] = turned[128:]

    loop(4, turn_targets)

    def weigh(k, held):
        return held + jnp.sum(kern[rows_at(k, 64), :].astype(F32), axis=0, keepdims=True)

    wr[o] = lax.fori_loop(0, 16, weigh, jnp.zeros((1, 512), F32))

    def project(h, values):
        def tile(k):
            cols = rows_at(k, 256)
            part[h, :, :, cols] = nn(values(), kern[:, cols]).reshape(16, 8, 256)

        loop(2, tile)

    def pair_up(h, step):
        return copy_to(
            part.at[h, pl.ds((1 - c) * 8, 8)], pair_in.at[h, step], pair_s.at[h, step], pair_r.at[h, step], sibling
        )

    def pairs(h, step):
        pair_up(h, step).wait()

        def add(z):
            chip[h, z] = part[h, c * 8 + z] + pair_in[h, step, z]

        loop(8, add)

    def along_line(src, dst, send, recv):
        def go(k):
            z = lax.rem(zl + k + 1, 8)
            copy_to(src.at[z], dst.at[zl], send.at[z], recv.at[zl], line(z)).start()

        loop(7, go)

    def line_arrived(src, dst, send, recv):
        def take(k):
            z = lax.rem(zl + k + 1, 8)
            copy_to(src.at[z], dst.at[z], send.at[z], recv.at[z], line(z)).wait()

        loop(7, take)

    def line_sum(src, dst):
        def add(k, held):
            return held + dst[lax.rem(zl + k + 1, 8)].astype(F32)

        return lax.fori_loop(0, 7, add, src[zl].astype(F32))

    def share_columns(h, step, after):
        buf, send, recv = vec.at[h, step], ag_s.at[h, step], ag_r.at[h, step]
        pair_send, pair_recv = sib_s.at[h, step], sib_r.at[h, step]
        mine = buf.at[o]

        def go(k):
            z = lax.rem(zl + k + 1, 8)
            copy_to(mine, mine, send.at[z], recv.at[zl], line(z)).start()

        loop(7, go)
        copy_to(mine, mine, pair_send.at[zl], pair_recv.at[zl], sibling).start()
        after()
        yield

        def relay(k):
            z = lax.rem(zl + k + 1, 8)
            piece = buf.at[c * 8 + z]
            copy_to(piece, piece, send.at[z], recv.at[z], line(z)).wait_recv()
            copy_to(piece, piece, pair_send.at[z], pair_recv.at[z], sibling).start()

        loop(7, relay)
        yield

        def from_sibling(z):
            piece = buf.at[(1 - c) * 8 + z]
            copy_to(piece, piece, pair_send.at[z], pair_recv.at[z], sibling).wait()

        loop(8, from_sibling)

        def sent(k):
            z = lax.rem(zl + k + 1, 8)
            copy_to(mine, mine, send.at[z], recv.at[z], line(z)).wait_send()

        loop(7, sent)

    def broadcast(src, dst, me, send, recv, where):
        def go(k):
            p = lax.rem(me + k + 1, 16)
            copy_to(src, dst.at[me], send.at[p], recv.at[me], where(p)).start()

        loop(15, go)

    def scatter(src, dst, me, send, recv, where):
        def go(k):
            p = lax.rem(me + k + 1, 16)
            copy_to(src.at[p], dst.at[me], send.at[p], recv.at[me], where(p)).start()

        loop(15, go)

    def gathered(dst, me, send, recv, where):
        def take(k):
            p = lax.rem(me + k + 1, 16)
            copy_to(dst.at[p], dst.at[p], send.at[p], recv.at[p], where(p)).wait()

        loop(15, take)

    def center_start(h, step, *columns):
        snr[h, step, xy] = to_row(*columns)
        broadcast(snr.at[h, step, xy], snr.at[h, step], xy, sn_s.at[h, step], sn_r.at[h, step], plane)

    def center_cross(h, step):
        return copy_to(scn.at[h, step, 0], scn.at[h, step, 1], sc_s.at[h, step], sc_r.at[h, step], across)

    def center_middle(h, step):
        gathered(snr.at[h, step], xy, sn_s.at[h, step], sn_r.at[h, step], plane)
        scn[h, step, 0] = jnp.sum(snr[h, step].reshape(16, 128), axis=0, keepdims=True)
        center_cross(h, step).start()

    def center_end(h, step):
        center_cross(h, step).wait()
        return scn[h, step, 0] + scn[h, step, 1]

    def predict(h, step, in_plane, in_cross):
        def tile(k):
            cols = rows_at(k, 256)
            values = vec[h, step].reshape(128, 512)
            ps[h, step, :, :, cols] = nt(values, kern[cols, :]).astype(BF16).reshape(16, 8, 256)

        loop(4, tile)
        out, back, send, recv = ps.at[h, step], pr.at[h, step], xs_s.at[h, step], xs_r.at[h, step]
        scatter(out, back, xy, send, recv, plane)
        in_plane()
        yield
        gathered(back, xy, send, recv, plane)

        def add(k, held):
            return held + pr[h, step, lax.rem(xy + k + 1, 16)].astype(F32)

        hs[h, step] = lax.fori_loop(0, 15, add, ps[h, step, xy].astype(F32)).astype(BF16)
        cross = copy_to(hs.at[h, step], hr.at[h, step], cr_s.at[h, step], cr_r.at[h, step], across)
        cross.start()
        in_cross()
        yield
        cross.wait()
        ph[h, step, xy] = (hs[h, step].astype(F32) + hr[h, step].astype(F32)).astype(BF16)
        whole, send, recv = ph.at[h, step], xg_s.at[h, step], xg_r.at[h, step]
        broadcast(whole.at[xy], whole, xy, send, recv, plane)
        yield
        gathered(whole, xy, send, recv, plane)

    waiting = [lambda: gathered(wr, o, w_s, w_r, any_dp)]

    def image_of(h, step):
        project(h, lambda: ph[h, step].reshape(128, 1024))

        def deflate(p):
            block = ph[h, step, p].astype(F32)
            middle = total(block) * (1.0 / block.shape[1])
            sts[h, step, p] = to_row(total(block * block), middle)
            part[h, p] = part[h, p] - middle * wr[o]

        loop(16, deflate)
        pair_up(h, 1 + step).start()
        str_[h, step, o] = sts[h, step, o]
        stats = str_.at[h, step], o, st_s.at[h, step], st_r.at[h, step], any_dp
        scatter(sts.at[h, step], *stats)
        yield
        pairs(h, 1 + step)

        def narrow(z):
            rems[h, step, z] = chip[h, z].astype(BF16)

        loop(8, narrow)
        moved = rems.at[h, step], remr.at[h, step], rem_s.at[h, step], rem_r.at[h, step]
        along_line(*moved)
        yield
        while waiting:
            waiting.pop()()
        gathered(*stats)

        def add(p, held):
            return held + str_[h, step, p]

        squares = from_row(lax.fori_loop(0, 16, add, jnp.zeros((1, 128), F32)), 0)

        def lift(p, held):
            return held + from_row(str_[h, step, p], 1) * wr[p]

        lifted = lax.fori_loop(0, 16, lift, jnp.zeros((8, 512), F32))
        line_arrived(*moved)
        summed = line_sum(moved[0], moved[1]) + lifted
        return summed * (1.0 / n_total), squares * (1.0 / n_total)

    def chain(h):
        project(h, lambda: tt[h])
        yield
        pair_up(h, 0).start()
        yield
        pairs(h, 0)

        def split(z):
            high = chip[h, z].astype(BF16)
            his[h, z] = high
            los[h, z] = (chip[h, z] - high.astype(F32)).astype(BF16)

        loop(8, split)
        highs = his.at[h], hir.at[h], hi_s.at[h], hi_r.at[h]
        lows = los.at[h], lor.at[h], lo_s.at[h], lo_r.at[h]
        along_line(*highs)
        yield
        line_arrived(*highs)
        bacc[h] = line_sum(highs[0], highs[1])
        vec[h, 0, o] = (bacc[h] * unscale).astype(BF16)
        yield from share_columns(h, 0, lambda: along_line(*lows))

        def finish_right_side():
            line_arrived(*lows)
            bacc[h] = (bacc[h] + line_sum(lows[0], lows[1])) * unscale
            center_start(h, 0, total(bacc[h] * bacc[h]))

        yield from predict(h, 0, finish_right_side, lambda: center_middle(h, 0))
        summed, squares = yield from image_of(h, 0)
        norm = from_row(center_end(h, 0), 0)
        image = summed + 0.5 * bacc[h]
        guess = norm / (squares + 0.5 * norm + EPS)
        near = bacc[h] - guess * image
        dacc[h] = image
        center_start(h, 1, total(bacc[h] * image), total(near * near), total(near * image), total(image * image))
        yield
        center_middle(h, 1)
        yield
        sums = center_end(h, 1)
        step_0 = norm / (from_row(sums, 0) + EPS)
        off = step_0 - guess
        norm_1 = from_row(sums, 1) - 2.0 * off * from_row(sums, 2) + off * off * from_row(sums, 3)
        racc[h] = bacc[h] - step_0 * dacc[h]
        dacc[h] = racc[h] + norm_1 / (norm + EPS) * bacc[h]
        vec[h, 1, o] = dacc[h].astype(BF16)
        yield from share_columns(h, 1, lambda: center_start(h, 2, total(dacc[h] * dacc[h])))
        yield from predict(h, 1, lambda: center_middle(h, 2), lambda: None)
        summed, squares = yield from image_of(h, 1)
        image = summed + 0.5 * dacc[h]
        step_1 = norm_1 / (squares + 0.5 * from_row(center_end(h, 2), 0) + EPS)
        vec[h, 2, o] = (racc[h] - step_1 * image).astype(BF16)
        finr[h, o] = to_row(step_0, step_1)
        final = finr.at[h], o, fin_s.at[h], fin_r.at[h], any_dp
        yield from share_columns(h, 2, lambda: broadcast(finr.at[h, o], *final))
        gathered(*final)

        def finish(p):
            first, second = from_row(finr[h, p], 0), from_row(finr[h, p], 1)
            part[h, p] = first * vec[h, 0, p].astype(F32) + second * vec[h, 1, p].astype(F32)

        loop(16, finish)

        def turn(k):
            rows = rows_at(k, 128)
            cols = pl.ds(h * 128, 128)
            coef_ref[rows, cols] = jnp.transpose(part[h, :, :, rows].reshape(128, 128))
            res_ref[rows, cols] = jnp.transpose(vec[h, 2, :, :, rows].astype(F32).reshape(128, 128))

        loop(4, turn)

    chains = [chain(0), chain(1)]
    for half in chains:
        next(half)
    pl.semaphore_wait(barrier, 31)
    started = False
    while chains:
        for half in list(chains):
            if next(half, "done") == "done":
                chains.remove(half)
        if not started:
            broadcast(wr.at[o], wr, o, w_s, w_r, any_dp)
            started = True


def on_device(features, centers, targets):
    n_total = features.shape[0] * lax.axis_size("dp")
    vmem, dma = pltpu.VMEM, pltpu.SemaphoreType.DMA
    whole = pl.BlockSpec(memory_space=pltpu.VMEM)
    out = jax.ShapeDtypeStruct((centers.shape[0], targets.shape[1]), F32)
    buffers = [
        vmem((1024, 1024), BF16), vmem((512, 1024), BF16), vmem((1024, 256), BF16),
        vmem((1024, 512), BF16), vmem((2, 128, 1024), BF16), vmem((2, 16, 8, 512), F32), vmem((2, 8, 8, 512), F32),
        vmem((2, 3, 8, 8, 512), F32), vmem((2, 8, 8, 512), BF16), vmem((2, 8, 8, 512), BF16),
        vmem((2, 8, 8, 512), BF16), vmem((2, 8, 8, 512), BF16), vmem((2, 3, 16, 8, 512), BF16),
        vmem((2, 2, 16, 8, 1024), BF16), vmem((2, 2, 16, 8, 1024), BF16),
        vmem((2, 2, 8, 1024), BF16), vmem((2, 2, 8, 1024), BF16), vmem((2, 2, 16, 8, 1024), BF16),
        vmem((2, 2, 16, 1, 128), F32), vmem((2, 2, 16, 1, 128), F32), vmem((16, 1, 512), F32),
        vmem((2, 2, 8, 8, 512), BF16), vmem((2, 2, 8, 8, 512), BF16),
        vmem((2, 3, 16, 1, 128), F32), vmem((2, 3, 2, 1, 128), F32), vmem((2, 16, 1, 128), F32),
        vmem((2, 8, 512), F32), vmem((2, 8, 512), F32), vmem((2, 8, 512), F32),
        dma((4,)), dma, dma,
    ]
    semaphores = []
    for shape in (
        (2, 3), (2, 8), (2, 8), (2, 3, 8), (2, 3, 8), (2, 2, 16), (2, 2), (2, 2, 16), (2, 2, 16), (16,),
        (2, 2, 8), (2, 3, 16), (2, 3), (2, 16),
    ):
        semaphores += [dma(shape), dma(shape)]
    return pl.pallas_call(
        functools.partial(kernel, n_total),
        out_shape=(out, out),
        in_specs=[pl.BlockSpec(memory_space=pl.ANY)] * 3,
        out_specs=(whole, whole),
        scratch_shapes=buffers + semaphores,
        compiler_params=pltpu.CompilerParams(
            collective_id=0, has_side_effects=True, vmem_limit_bytes=60 * 1024 * 1024
        ),
    )(features, centers, targets)


def solution(mesh):
    placed = (P("dp", None), P("center", None), P("dp", None))
    return jax.shard_map(
        on_device,
        mesh=mesh,
        in_specs=placed,
        out_specs=(P("center", None), P("center", None)),
        check_vma=False,
    )
```

time: 157 us -> 155 us (0.987)
  local copies, waits for them, and re-layouts: 5.44 us -> 3.74 us
    unnamed x8 -> x2, local copies, waits for them, and re-layouts: 5.44 us -> 3.74 us
where the time goes in v2:
time: 155 us; the launch traced here: 154 us
  Pallas kernels  150 us (97%)
  local copies, waits for them, and re-layouts  3.74 us (2%)
    pallas_call x1, Pallas kernels, on_device(): pl.pallas_call(functools.partial(kernel, n_total), out_shape=(out, out),...  150 us
    unnamed x2, local copies, waits for them, and re-layouts  3.74 us

profile of v2, /device:TPU:1, one launch (start us, length us, event | category | flops | bytes accessed | tf_op | source)
XLA Modules:
  0.0 154.2 jit_solution(12737951157505617272)
XLA Ops:
  0.6 149.9 %shard_map.50 = (f32[512,256]{1,0:T(8,128)}, f32[512,256]{1,0:T(8,128)}) custom-call(bf16[1024,1024]{1,0:T(8,128)(2,1)} %f_hbm.1, bf16[512,1024]{1,0:T(8,128)(2,1)} %c_hbm.1, bf16[1024,256]{1,0:T(8,128)(2,1)} %t_hbm.1), custom_call_target="tpu_custom_call" | custom-call | tf_op jit(solution)/shard_map/pallas_call | solution.py:426
  150.5 1.9 %copy.7 = f32[512,256]{1,0:T(8,128)} copy(f32[512,256]{1,0:T(8,128)} %get-tuple-element.4) | data formatting | bytes 1048576
  152.4 1.9 %copy.8 = f32[512,256]{1,0:T(8,128)} copy(f32[512,256]{1,0:T(8,128)} %get-tuple-element.5) | data formatting | bytes 1048576

commit v3 on v2

v3 whole, which is shorter than its diff:
```python
import functools
import math

import jax
import jax.numpy as jnp
from jax import lax
from jax.experimental import pallas as pl
from jax.experimental.pallas import tpu as pltpu
from jax.sharding import PartitionSpec as P

MESH = pl.DeviceIdType.MESH
F32, BF16 = jnp.float32, jnp.bfloat16
EPS = 1e-06
FIRST = 2


def nt(a, b):
    return lax.dot_general(a, b, (((1,), (1,)), ((), ())), preferred_element_type=F32)


def nn(a, b):
    return lax.dot_general(a, b, (((1,), (0,)), ((), ())), preferred_element_type=F32)


def total(x):
    return jnp.sum(x, axis=1, keepdims=True)


def diagonal(slot):
    lane = lax.broadcasted_iota(jnp.int32, (16, 128), 1)
    return lane == lax.broadcasted_iota(jnp.int32, (16, 128), 0) + 16 * slot


def to_row(*columns):
    held = jnp.zeros((16, 128), F32)
    for slot, column in enumerate(columns):
        held = jnp.where(diagonal(slot), column, held)
    return jnp.sum(held, axis=0, keepdims=True)


def from_row(row, slot):
    return total(jnp.where(diagonal(slot), jnp.broadcast_to(row, (16, 128)), 0.0))


def to_rows(*columns):
    held = jnp.zeros((8, 16, 128), F32)
    for slot, column in enumerate(columns):
        held = jnp.where(diagonal(slot)[None], column, held)
    return jnp.sum(held, axis=1, keepdims=True)


def from_rows(rows, slot):
    spread = jnp.where(diagonal(slot)[None], jnp.broadcast_to(rows, (rows.shape[0], 16, 128)), 0.0)
    return jnp.sum(spread, axis=2, keepdims=True)


def copy_to(src, dst, send, recv, where):
    return pltpu.make_async_remote_copy(
        src_ref=src, dst_ref=dst, send_sem=send, recv_sem=recv, device_id=where, device_id_type=MESH
    )


def loop(count, body):
    def step(k, carry):
        body(k)
        return carry

    lax.fori_loop(0, count, step, 0)


def kernel(
    n_total, f_hbm, c_hbm, t_hbm, coef_ref, res_ref,
    f_ref, c_ref, t_ref, kern, flip, tt, part, pair_in, his, hir, los, lor, vec,
    ps, pr, hs, hr, ph, sts, str_, wr, rems, remr, snr, scn, finr, bacc, dacc, racc, held,
    load_f, load_c, load_t,
    pair_s, pair_r, hi_s, hi_r, lo_s, lo_r, ag_s, ag_r, sib_s, sib_r,
    xs_s, xs_r, cr_s, cr_r, xg_s, xg_r, st_s, st_r, w_s, w_r, rem_s, rem_r, sn_s, sn_r, sc_s, sc_r, fin_s, fin_r,
):
    g, j = lax.axis_index("dp"), lax.axis_index("center")
    zl, c = lax.div(g, 2), lax.rem(g, 2)
    xy, zh = lax.div(j, 2), lax.rem(j, 2)
    me = c * 8 + zl
    owning = jnp.logical_and(zl >= FIRST, zl < FIRST + 4)
    seat = lax.clamp(0, zl - FIRST, 3)
    o = c * 4 + seat
    sibling = (zl * 2 + (1 - c), j)
    across = (g, xy * 2 + (1 - zh))

    def line(z):
        return (z * 2 + c, j)

    def any_dp(p):
        return (lax.rem(p, 8) * 2 + lax.div(p, 8), j)

    def owner_at(q):
        return lax.div(q, 4) * 8 + FIRST + lax.rem(q, 4)

    def plane(p):
        return (g, p * 2 + zh)

    barrier = pltpu.get_barrier_semaphore()

    def greet(where):
        pl.semaphore_signal(barrier, inc=1, device_id=where, device_id_type=MESH)

    greet(across)
    loop(15, lambda k: greet(any_dp(lax.rem(me + k + 1, 16))))
    loop(15, lambda k: greet(plane(lax.rem(xy + k + 1, 16))))

    scale = 0.5 / math.sqrt(f_ref.shape[1])
    unscale = 1.0 / math.sqrt(n_total)
    quarter = f_ref.shape[0] // 4

    def rows_at(k, size):
        return pl.ds(pl.multiple_of(k * size, size), size)

    def load(k):
        return pltpu.make_async_copy(f_hbm.at[rows_at(k, quarter)], f_ref.at[rows_at(k, quarter)], load_f.at[k])

    centers_in = pltpu.make_async_copy(c_hbm, c_ref, load_c)
    targets_in = pltpu.make_async_copy(t_hbm, t_ref, load_t)
    centers_in.start()
    loop(4, lambda k: load(k).start())
    targets_in.start()
    centers_in.wait()

    def kernel_rows(k):
        load(k).wait()
        rows = rows_at(k, quarter)

        def tile(i):
            cols = rows_at(i, 256)
            lifted = 1.0 + scale * nt(f_ref[rows, :], c_ref[cols, :])
            cubed = lifted * lifted * lifted
            kern[rows, cols] = cubed.astype(BF16)
            flip[cols, rows] = jnp.transpose(cubed).astype(BF16)

        loop(2, tile)

    loop(4, kernel_rows)
    targets_in.wait()

    def turn_targets(k):
        at = rows_at(k, 256)
        turned = jnp.transpose(t_ref[at, :].astype(F32)).astype(BF16)
        tt[0, :, at] = turned[:128]
        tt[1, :, at] = turned[128:]

    loop(4, turn_targets)

    def weigh(k, held):
        return held + jnp.sum(kern[rows_at(k, 64), :].astype(F32), axis=0, keepdims=True)

    wr[me] = lax.fori_loop(0, 16, weigh, jnp.zeros((1, 512), F32))

    def project(h, values):
        def tile(k):
            cols = rows_at(k, 256)
            part[h, :, :, cols] = nn(values(), kern[:, cols]).reshape(8, 16, 256)

        loop(2, tile)

    def pair_up(h, step):
        return copy_to(
            part.at[h, pl.ds((1 - c) * 4, 4)], pair_in.at[h, step], pair_s.at[h, step], pair_r.at[h, step], sibling
        )

    def pairs(h, step):
        pair_up(h, step).wait()
        return part[h, pl.ds(c * 4, 4)] + pair_in[h, step]

    def others(count, first, body):
        def visit(k):
            z = first + k

            @pl.when(z != zl)
            def _():
                body(k, z)

        loop(count, visit)

    def to_owners(src, dst, send, recv):
        def go(k, z):
            copy_to(src.at[k], dst.at[zl], send.at[k], recv.at[zl], line(z)).start()

        others(4, FIRST, go)

    def owners_took(src, dst, send, recv):
        def gone(k, z):
            copy_to(src.at[k], dst.at[zl], send.at[k], recv.at[zl], line(z)).wait_send()

        others(4, FIRST, gone)

    def line_sum(src, dst, send, recv):
        def take(k, z):
            copy_to(dst.at[z], dst.at[z], send.at[0], recv.at[z], line(z)).wait_recv()

        others(8, 0, take)
        dst[zl] = src[seat]
        return jnp.sum(dst[...].astype(F32), axis=0)

    def share_columns(h, step, after):
        buf, send, recv = vec.at[h, step], ag_s.at[h, step], ag_r.at[h, step]
        pair_send, pair_recv = sib_s.at[h, step], sib_r.at[h, step]
        mine = buf.at[o]

        @pl.when(owning)
        def _():
            def go(k, z):
                copy_to(mine, mine, send.at[z], recv.at[seat], line(z)).start()

            others(8, 0, go)
            copy_to(mine, mine, pair_send.at[seat], pair_recv.at[seat], sibling).start()
            after()

        yield

        def relay(k, z):
            piece = buf.at[c * 4 + k]
            copy_to(piece, piece, send.at[z], recv.at[k], line(z)).wait_recv()
            copy_to(piece, piece, pair_send.at[k], pair_recv.at[k], sibling).start()

        others(4, FIRST, relay)
        yield

        def from_sibling(k):
            piece = buf.at[(1 - c) * 4 + k]
            copy_to(piece, piece, pair_send.at[k], pair_recv.at[k], sibling).wait()

        loop(4, from_sibling)

        @pl.when(owning)
        def _():
            def sent(k, z):
                copy_to(mine, mine, send.at[z], recv.at[seat], line(z)).wait_send()

            others(8, 0, sent)

    def tell_owners(src, dst, send, recv):
        def go(q):
            p = owner_at(q)

            @pl.when(p != me)
            def _():
                copy_to(src(q), dst.at[me], send.at[q], recv.at[me], any_dp(p)).start()

        loop(8, go)

    def owners_told(src, dst, send, recv):
        def gone(q):
            p = owner_at(q)

            @pl.when(p != me)
            def _():
                copy_to(src(q), dst.at[me], send.at[q], recv.at[me], any_dp(p)).wait_send()

        loop(8, gone)

        @pl.when(owning)
        def _():
            def take(k):
                p = lax.rem(me + k + 1, 16)
                copy_to(dst.at[p], dst.at[p], send.at[0], recv.at[p], any_dp(p)).wait_recv()

            loop(15, take)

    def broadcast(src, dst, own, send, recv, where):
        def go(k):
            p = lax.rem(own + k + 1, 16)
            copy_to(src, dst.at[own], send.at[p], recv.at[own], where(p)).start()

        loop(15, go)

    def scatter(src, dst, own, send, recv, where):
        def go(k):
            p = lax.rem(own + k + 1, 16)
            copy_to(src.at[p], dst.at[own], send.at[p], recv.at[own], where(p)).start()

        loop(15, go)

    def gathered(dst, own, send, recv, where):
        def take(k):
            p = lax.rem(own + k + 1, 16)
            copy_to(dst.at[p], dst.at[p], send.at[p], recv.at[p], where(p)).wait()

        loop(15, take)

    def center_start(h, step, *columns):
        snr[h, step, xy] = to_row(*columns)
        broadcast(snr.at[h, step, xy], snr.at[h, step], xy, sn_s.at[h, step], sn_r.at[h, step], plane)

    def center_cross(h, step):
        return copy_to(scn.at[h, step, 0], scn.at[h, step, 1], sc_s.at[h, step], sc_r.at[h, step], across)

    def center_middle(h, step):
        gathered(snr.at[h, step], xy, sn_s.at[h, step], sn_r.at[h, step], plane)
        scn[h, step, 0] = jnp.sum(snr[h, step].reshape(16, 128), axis=0, keepdims=True)
        center_cross(h, step).start()

    def center_end(h, step):
        center_cross(h, step).wait()
        return scn[h, step, 0] + scn[h, step, 1]

    def predict(h, step, in_plane, in_cross):
        def tile(k):
            cols = rows_at(k, 256)
            values = vec[h, step].reshape(128, 512)
            ps[h, step, :, :, cols] = nn(values, flip[:, cols]).astype(BF16).reshape(16, 8, 256)

        loop(4, tile)
        out, back, send, recv = ps.at[h, step], pr.at[h, step], xs_s.at[h, step], xs_r.at[h, step]
        scatter(out, back, xy, send, recv, plane)
        in_plane()
        yield
        gathered(back, xy, send, recv, plane)

        pr[h, step, xy] = ps[h, step, xy]
        hs[h, step] = jnp.sum(pr[h, step].astype(F32), axis=0).astype(BF16)
        cross = copy_to(hs.at[h, step], hr.at[h, step], cr_s.at[h, step], cr_r.at[h, step], across)
        cross.start()
        in_cross()
        yield
        cross.wait()
        ph[h, step, xy] = (hs[h, step].astype(F32) + hr[h, step].astype(F32)).astype(BF16)
        whole, send, recv = ph.at[h, step], xg_s.at[h, step], xg_r.at[h, step]
        broadcast(whole.at[xy], whole, xy, send, recv, plane)
        yield
        gathered(whole, xy, send, recv, plane)

    weights = lambda q: wr.at[me], wr, w_s, w_r
    waiting = [lambda: owners_told(*weights)]

    def keep(h, slot, value):
        held[h, slot] = jnp.broadcast_to(value, (16, 128))

    def kept(h, slot):
        return held[h, slot][:, :1]

    def image_of(h, step, use):
        project(h, lambda: ph[h, step].reshape(128, 1024))
        block = ph[h, step].astype(F32).reshape(8, 16, 1024)
        middle = jnp.sum(block, axis=2, keepdims=True) * (1.0 / block.shape[2])
        sts[h, step] = to_rows(jnp.sum(block * block, axis=2, keepdims=True), middle)
        part[h] = part[h] - middle * wr[me][None]
        pair_up(h, 1 + step).start()
        told = str_.at[h, step]
        stats = lambda q: sts.at[h, step, q], told, st_s.at[h, step], st_r.at[h, step]
        tell_owners(*stats)
        yield
        rems[h, step] = pairs(h, 1 + step).astype(BF16)
        moved = rems.at[h, step], remr.at[h, step], rem_s.at[h, step], rem_r.at[h, step]
        to_owners(*moved)
        yield
        while waiting:
            waiting.pop()()
        owners_told(*stats)

        @pl.when(owning)
        def _():
            told[me] = sts[h, step, o]
            rows = told[...]
            squares = from_row(jnp.sum(rows, axis=0), 0)
            lifted = jnp.sum(from_rows(rows, 1) * wr[...], axis=0)
            use((line_sum(*moved) + lifted) * (1.0 / n_total), squares * (1.0 / n_total))

        owners_took(*moved)

    def chain(h):
        project(h, lambda: tt[h])
        yield
        pair_up(h, 0).start()
        yield
        both = pairs(h, 0)
        high = both.astype(BF16)
        his[h] = high
        los[h] = (both - high.astype(F32)).astype(BF16)
        highs = his.at[h], hir.at[h], hi_s.at[h], hi_r.at[h]
        lows = los.at[h], lor.at[h], lo_s.at[h], lo_r.at[h]
        to_owners(*highs)
        yield

        @pl.when(owning)
        def _():
            bacc[h] = line_sum(*highs)
            vec[h, 0, o] = (bacc[h] * unscale).astype(BF16)

        yield from share_columns(h, 0, lambda: None)
        owners_took(*highs)

        def finish_right_side():
            @pl.when(owning)
            def _():
                bacc[h] = (bacc[h] + line_sum(*lows)) * unscale
                center_start(h, 0, total(bacc[h] * bacc[h]))

            owners_took(*lows)

        yield from predict(h, 0, lambda: to_owners(*lows), finish_right_side)

        def open_first(summed, squares):
            norm = from_row(center_end(h, 0), 0)
            image = summed + 0.5 * bacc[h]
            guess = norm / (squares + 0.5 * norm + EPS)
            near = bacc[h] - guess * image
            dacc[h] = image
            keep(h, 0, norm)
            keep(h, 1, guess)
            center_start(h, 1, total(bacc[h] * image), total(near * near), total(near * image), total(image * image))

        pl.when(owning)(lambda: center_middle(h, 0))
        yield from image_of(h, 0, open_first)
        yield
        pl.when(owning)(lambda: center_middle(h, 1))
        yield

        @pl.when(owning)
        def _():
            sums = center_end(h, 1)
            norm, guess = kept(h, 0), kept(h, 1)
            step_0 = norm / (from_row(sums, 0) + EPS)
            off = step_0 - guess
            norm_1 = from_row(sums, 1) - 2.0 * off * from_row(sums, 2) + off * off * from_row(sums, 3)
            racc[h] = bacc[h] - step_0 * dacc[h]
            dacc[h] = racc[h] + norm_1 / (norm + EPS) * bacc[h]
            vec[h, 1, o] = dacc[h].astype(BF16)
            keep(h, 2, step_0)
            keep(h, 3, norm_1)

        yield from share_columns(h, 1, lambda: center_start(h, 2, total(dacc[h] * dacc[h])))
        yield from predict(h, 1, lambda: pl.when(owning)(lambda: center_middle(h, 2)), lambda: None)
        send_all, recv_all = fin_s.at[h], fin_r.at[h]

        def close(summed, squares):
            image = summed + 0.5 * dacc[h]
            step_1 = kept(h, 3) / (squares + 0.5 * from_row(center_end(h, 2), 0) + EPS)
            vec[h, 2, o] = (racc[h] - step_1 * image).astype(BF16)
            finr[h, o] = to_row(kept(h, 2), step_1)

        def announce():
            def go(k):
                p = lax.rem(me + k + 1, 16)
                copy_to(finr.at[h, o], finr.at[h, o], send_all.at[p], recv_all.at[o], any_dp(p)).start()

            loop(15, go)

        yield from image_of(h, 1, close)
        yield from share_columns(h, 2, announce)

        def hear(q):
            p = owner_at(q)

            @pl.when(p != me)
            def _():
                copy_to(finr.at[h, q], finr.at[h, q], send_all.at[p], recv_all.at[q], any_dp(p)).wait_recv()

        loop(8, hear)

        @pl.when(owning)
        def _():
            def sent(k):
                p = lax.rem(me + k + 1, 16)
                copy_to(finr.at[h, o], finr.at[h, o], send_all.at[p], recv_all.at[o], any_dp(p)).wait_send()

            loop(15, sent)

        first, second = from_rows(finr[h], 0), from_rows(finr[h], 1)
        part[h] = first * vec[h, 0].astype(F32) + second * vec[h, 1].astype(F32)

        def turn(k):
            rows = rows_at(k, 128)
            cols = pl.ds(h * 128, 128)
            coef_ref[rows, cols] = jnp.transpose(part[h, :, :, rows].reshape(128, 128))
            res_ref[rows, cols] = jnp.transpose(vec[h, 2, :, :, rows].astype(F32).reshape(128, 128))

        loop(4, turn)

    chains = [chain(0), chain(1)]
    for half in chains:
        next(half)
    pl.semaphore_wait(barrier, 31)
    started = False
    while chains:
        for half in list(chains):
            if next(half, "done") == "done":
                chains.remove(half)
        if not started:
            tell_owners(*weights)
            started = True


def on_device(features, centers, targets):
    n_total = features.shape[0] * lax.axis_size("dp")
    vmem, dma = pltpu.VMEM, pltpu.SemaphoreType.DMA
    whole = pl.BlockSpec(memory_space=pltpu.VMEM)
    out = jax.ShapeDtypeStruct((centers.shape[0], targets.shape[1]), F32)
    buffers = [
        vmem((1024, 1024), BF16), vmem((512, 1024), BF16), vmem((1024, 256), BF16),
        vmem((1024, 512), BF16), vmem((512, 1024), BF16), vmem((2, 128, 1024), BF16), vmem((2, 8, 16, 512), F32),
        vmem((2, 3, 4, 16, 512), F32), vmem((2, 4, 16, 512), BF16), vmem((2, 8, 16, 512), BF16),
        vmem((2, 4, 16, 512), BF16), vmem((2, 8, 16, 512), BF16), vmem((2, 3, 8, 16, 512), BF16),
        vmem((2, 2, 16, 8, 1024), BF16), vmem((2, 2, 16, 8, 1024), BF16),
        vmem((2, 2, 8, 1024), BF16), vmem((2, 2, 8, 1024), BF16), vmem((2, 2, 16, 8, 1024), BF16),
        vmem((2, 2, 8, 1, 128), F32), vmem((2, 2, 16, 1, 128), F32), vmem((16, 1, 512), F32),
        vmem((2, 2, 4, 16, 512), BF16), vmem((2, 2, 8, 16, 512), BF16),
        vmem((2, 3, 16, 1, 128), F32), vmem((2, 3, 2, 1, 128), F32), vmem((2, 8, 1, 128), F32),
        vmem((2, 16, 512), F32), vmem((2, 16, 512), F32), vmem((2, 16, 512), F32), vmem((2, 4, 16, 128), F32),
        dma((4,)), dma, dma,
    ]
    semaphores = []
    for send, recv in (
        ((2, 3), (2, 3)), ((2, 4), (2, 8)), ((2, 4), (2, 8)), ((2, 3, 8), (2, 3, 4)), ((2, 3, 4), (2, 3, 4)),
        ((2, 2, 16), (2, 2, 16)), ((2, 2), (2, 2)), ((2, 2, 16), (2, 2, 16)), ((2, 2, 8), (2, 2, 16)), ((8,), (16,)),
        ((2, 2, 4), (2, 2, 8)), ((2, 3, 16), (2, 3, 16)), ((2, 3), (2, 3)), ((2, 16), (2, 8)),
    ):
        semaphores += [dma(send), dma(recv)]
    return pl.pallas_call(
        functools.partial(kernel, n_total),
        out_shape=(out, out),
        in_specs=[pl.BlockSpec(memory_space=pl.ANY)] * 3,
        out_specs=(whole, whole),
        scratch_shapes=buffers + semaphores,
        compiler_params=pltpu.CompilerParams(
            collective_id=0, has_side_effects=True, vmem_limit_bytes=60 * 1024 * 1024
        ),
    )(features, centers, targets)


def solution(mesh):
    placed = (P("dp", None), P("center", None), P("dp", None))
    return jax.shard_map(
        on_device,
        mesh=mesh,
        in_specs=placed,
        out_specs=(P("center", None), P("center", None)),
        check_vma=False,
    )
```

time: 155 us -> 142 us (0.916)
  Pallas kernels: 150 us -> 138 us
    pallas_call x1, Pallas kernels: 150 us -> 138 us  [on_device(): pl.pallas_call(functools.partial(kernel, n_total), out_shape=(out, out),...]
where the time goes in v3:
time: 142 us
  Pallas kernels  138 us (97%)
  local copies, waits for them, and re-layouts  3.74 us (3%)
    pallas_call x1, Pallas kernels, on_device(): pl.pallas_call(functools.partial(kernel, n_total), out_shape=(out, out),...  138 us
    unnamed x2, local copies, waits for them, and re-layouts  3.74 us

profile of v3, /device:TPU:1, one launch (start us, length us, event | category | flops | bytes accessed | tf_op | source)
XLA Modules:
  0.0 141.9 jit_solution(668311712525326507)
XLA Ops:
  0.6 137.5 %shard_map.50 = (f32[512,256]{1,0:T(8,128)}, f32[512,256]{1,0:T(8,128)}) custom-call(bf16[1024,1024]{1,0:T(8,128)(2,1)} %f_hbm.1, bf16[512,1024]{1,0:T(8,128)(2,1)} %c_hbm.1, bf16[1024,256]{1,0:T(8,128)(2,1)} %t_hbm.1), custom_call_target="tpu_custom_call" | custom-call | tf_op jit(solution)/shard_map/pallas_call | solution.py:516
  138.2 1.9 %copy.7 = f32[512,256]{1,0:T(8,128)} copy(f32[512,256]{1,0:T(8,128)} %get-tuple-element.4) | data formatting | bytes 1048576
  140.0 1.9 %copy.8 = f32[512,256]{1,0:T(8,128)} copy(f32[512,256]{1,0:T(8,128)} %get-tuple-element.5) | data formatting | bytes 1048576

commit v4 on v3

--- a/solution.py
+++ b/solution.py
@@ -11,6 +11,9 @@
 MESH = pl.DeviceIdType.MESH
 F32, BF16 = jnp.float32, jnp.bfloat16
 EPS = 1e-06
+FAR_FIRST = sorted(
+    ((a, b) for a in range(4) for b in range(4) if a + b), key=lambda t: -min(t[0], 4 - t[0]) - min(t[1], 4 - t[1])
+)
 FIRST = 2
 
 
@@ -131,9 +134,7 @@
         def tile(i):
             cols = rows_at(i, 256)
             lifted = 1.0 + scale * nt(f_ref[rows, :], c_ref[cols, :])
-            cubed = lifted * lifted * lifted
-            kern[rows, cols] = cubed.astype(BF16)
-            flip[cols, rows] = jnp.transpose(cubed).astype(BF16)
+            kern[rows, cols] = (lifted * lifted * lifted).astype(BF16)
 
         loop(2, tile)
 
@@ -151,7 +152,14 @@
     def weigh(k, held):
         return held + jnp.sum(kern[rows_at(k, 64), :].astype(F32), axis=0, keepdims=True)
 
-    wr[me] = lax.fori_loop(0, 16, weigh, jnp.zeros((1, 512), F32))
+    def prepare():
+        def turn_kernel(k):
+            rows = rows_at(k, 128)
+            flip[:, rows] = jnp.transpose(kern[rows, :].astype(F32)).astype(BF16)
+
+        loop(8, turn_kernel)
+        wr[me] = lax.fori_loop(0, 16, weigh, jnp.zeros((1, 512), F32))
+        tell_owners(*weights)
 
     def project(h, values):
         def tile(k):
@@ -179,23 +187,36 @@
 
         loop(count, visit)
 
+    def farthest_first(reach, low, high, body):
+        def visit(k):
+            for z in (zl + reach - k, zl - reach + k):
+
+                @pl.when(jnp.logical_and(z >= low, z < high))
+                def _():
+                    body(z)
+
+        loop(reach, visit)
+
     def to_owners(src, dst, send, recv):
-        def go(k, z):
-            copy_to(src.at[k], dst.at[zl], send.at[k], recv.at[zl], line(z)).start()
-
-        others(4, FIRST, go)
+        def go(z):
+            k = z - FIRST
+            copy_to(src.at[k], dst.at[zl], send, recv, line(z)).start()
+
+        farthest_first(5, FIRST, FIRST + 4, go)
+
+    def sent_or_told(count, wait):
+        pl.when(owning)(lambda: wait(count - 1))
+        pl.when(jnp.logical_not(owning))(lambda: wait(count))
+
+    def many(ref, count, send, recv):
+        rows = ref.at[pl.ds(0, count)]
+        return copy_to(rows, rows, send, recv, sibling)
 
     def owners_took(src, dst, send, recv):
-        def gone(k, z):
-            copy_to(src.at[k], dst.at[zl], send.at[k], recv.at[zl], line(z)).wait_send()
-
-        others(4, FIRST, gone)
+        sent_or_told(4, lambda count: many(src, count, send, recv).wait_send())
 
     def line_sum(src, dst, send, recv):
-        def take(k, z):
-            copy_to(dst.at[z], dst.at[z], send.at[0], recv.at[z], line(z)).wait_recv()
-
-        others(8, 0, take)
+        many(dst, 7, send, recv).wait_recv()
         dst[zl] = src[seat]
         return jnp.sum(dst[...].astype(F32), axis=0)
 
@@ -206,35 +227,25 @@
 
         @pl.when(owning)
         def _():
-            def go(k, z):
-                copy_to(mine, mine, send.at[z], recv.at[seat], line(z)).start()
-
-            others(8, 0, go)
-            copy_to(mine, mine, pair_send.at[seat], pair_recv.at[seat], sibling).start()
+            def go(z):
+                copy_to(mine, mine, send, recv.at[seat], line(z)).start()
+
+            farthest_first(5, 0, 8, go)
+            copy_to(mine, mine, pair_send, pair_recv, sibling).start()
             after()
 
         yield
 
         def relay(k, z):
             piece = buf.at[c * 4 + k]
-            copy_to(piece, piece, send.at[z], recv.at[k], line(z)).wait_recv()
-            copy_to(piece, piece, pair_send.at[k], pair_recv.at[k], sibling).start()
+            copy_to(piece, piece, send, recv.at[k], line(z)).wait_recv()
+            copy_to(piece, piece, pair_send, pair_recv, sibling).start()
 
         others(4, FIRST, relay)
         yield
 
-        def from_sibling(k):
-            piece = buf.at[(1 - c) * 4 + k]
-            copy_to(piece, piece, pair_send.at[k], pair_recv.at[k], sibling).wait()
-
-        loop(4, from_sibling)
-
-        @pl.when(owning)
-        def _():
-            def sent(k, z):
-                copy_to(mine, mine, send.at[z], recv.at[seat], line(z)).wait_send()
-
-            others(8, 0, sent)
+        many(buf, 4, pair_send, pair_recv).wait()
+        pl.when(owning)(lambda: many(buf, 7, send, recv.at[0]).wait_send())
 
     def tell_owners(src, dst, send, recv):
         def go(q):
@@ -242,48 +253,28 @@
 
             @pl.when(p != me)
             def _():
-                copy_to(src(q), dst.at[me], send.at[q], recv.at[me], any_dp(p)).start()
+                copy_to(src(q), dst.at[me], send, recv, any_dp(p)).start()
 
         loop(8, go)
 
     def owners_told(src, dst, send, recv):
-        def gone(q):
-            p = owner_at(q)
-
-            @pl.when(p != me)
-            def _():
-                copy_to(src(q), dst.at[me], send.at[q], recv.at[me], any_dp(p)).wait_send()
-
-        loop(8, gone)
-
-        @pl.when(owning)
-        def _():
-            def take(k):
-                p = lax.rem(me + k + 1, 16)
-                copy_to(dst.at[p], dst.at[p], send.at[0], recv.at[p], any_dp(p)).wait_recv()
-
-            loop(15, take)
+        sent_or_told(8, lambda count: many(dst, count, send, recv).wait_send())
+        pl.when(owning)(lambda: many(dst, 15, send, recv).wait_recv())
+
+    def peers():
+        x, y = lax.div(xy, 4), lax.rem(xy, 4)
+        return [lax.rem(x + a, 4) * 4 + lax.rem(y + b, 4) for a, b in FAR_FIRST]
 
     def broadcast(src, dst, own, send, recv, where):
-        def go(k):
-            p = lax.rem(own + k + 1, 16)
-            copy_to(src, dst.at[own], send.at[p], recv.at[own], where(p)).start()
-
-        loop(15, go)
+        for p in peers():
+            copy_to(src, dst.at[own], send, recv, where(p)).start()
 
     def scatter(src, dst, own, send, recv, where):
-        def go(k):
-            p = lax.rem(own + k + 1, 16)
-            copy_to(src.at[p], dst.at[own], send.at[p], recv.at[own], where(p)).start()
-
-        loop(15, go)
+        for p in peers():
+            copy_to(src.at[p], dst.at[own], send, recv, where(p)).start()
 
     def gathered(dst, own, send, recv, where):
-        def take(k):
-            p = lax.rem(own + k + 1, 16)
-            copy_to(dst.at[p], dst.at[p], send.at[p], recv.at[p], where(p)).wait()
-
-        loop(15, take)
+        many(dst, 15, send, recv).wait()
 
     def center_start(h, step, *columns):
         snr[h, step, xy] = to_row(*columns)
@@ -439,29 +430,15 @@
         def announce():
             def go(k):
                 p = lax.rem(me + k + 1, 16)
-                copy_to(finr.at[h, o], finr.at[h, o], send_all.at[p], recv_all.at[o], any_dp(p)).start()
+                copy_to(finr.at[h, o], finr.at[h, o], send_all, recv_all, any_dp(p)).start()
 
             loop(15, go)
 
         yield from image_of(h, 1, close)
         yield from share_columns(h, 2, announce)
 
-        def hear(q):
-            p = owner_at(q)
-
-            @pl.when(p != me)
-            def _():
-                copy_to(finr.at[h, q], finr.at[h, q], send_all.at[p], recv_all.at[q], any_dp(p)).wait_recv()
-
-        loop(8, hear)
-
-        @pl.when(owning)
-        def _():
-            def sent(k):
-                p = lax.rem(me + k + 1, 16)
-                copy_to(finr.at[h, o], finr.at[h, o], send_all.at[p], recv_all.at[o], any_dp(p)).wait_send()
-
-            loop(15, sent)
+        sent_or_told(8, lambda count: many(finr.at[h], count, send_all, recv_all).wait_recv())
+        pl.when(owning)(lambda: many(snr.at[h, 0], 15, send_all, recv_all).wait_send())
 
         first, second = from_rows(finr[h], 0), from_rows(finr[h], 1)
         part[h] = first * vec[h, 0].astype(F32) + second * vec[h, 1].astype(F32)
@@ -478,14 +455,14 @@
     for half in chains:
         next(half)
     pl.semaphore_wait(barrier, 31)
-    started = False
+    turns = 0
     while chains:
         for half in list(chains):
             if next(half, "done") == "done":
                 chains.remove(half)
-        if not started:
-            tell_owners(*weights)
-            started = True
+        turns += 1
+        if turns == 2:
+            prepare()
 
 
 def on_device(features, centers, targets):
@@ -508,9 +485,9 @@
     ]
     semaphores = []
     for send, recv in (
-        ((2, 3), (2, 3)), ((2, 4), (2, 8)), ((2, 4), (2, 8)), ((2, 3, 8), (2, 3, 4)), ((2, 3, 4), (2, 3, 4)),
-        ((2, 2, 16), (2, 2, 16)), ((2, 2), (2, 2)), ((2, 2, 16), (2, 2, 16)), ((2, 2, 8), (2, 2, 16)), ((8,), (16,)),
-        ((2, 2, 4), (2, 2, 8)), ((2, 3, 16), (2, 3, 16)), ((2, 3), (2, 3)), ((2, 16), (2, 8)),
+        ((2, 3), (2, 3)), ((2,), (2,)), ((2,), (2,)), ((2, 3), (2, 3, 4)), ((2, 3), (2, 3)),
+        ((2, 2), (2, 2)), ((2, 2), (2, 2)), ((2, 2), (2, 2)), ((2, 2), (2, 2)), ((), ()),
+        ((2, 2), (2, 2)), ((2, 3), (2, 3)), ((2, 3), (2, 3)), ((2,), (2,)),
     ):
         semaphores += [dma(send), dma(recv)]
     return pl.pallas_call(

time: 142 us -> 132 us (0.930)
  Pallas kernels: 138 us -> 128 us
    pallas_call x1, Pallas kernels: 138 us -> 128 us  [on_device(): pl.pallas_call(functools.partial(kernel, n_total), out_shape=(out, out),...]
where the time goes in v4:
time: 132 us
  Pallas kernels  128 us (97%)
  local copies, waits for them, and re-layouts  3.74 us (3%)
    pallas_call x1, Pallas kernels, on_device(): pl.pallas_call(functools.partial(kernel, n_total), out_shape=(out, out),...  128 us
    unnamed x2, local copies, waits for them, and re-layouts  3.74 us

profile of v4, /device:TPU:1, one launch (start us, length us, event | category | flops | bytes accessed | tf_op | source)
XLA Modules:
  0.0 132.1 jit_solution(7118364561712326661)
XLA Ops:
  0.6 127.8 %shard_map.50 = (f32[512,256]{1,0:T(8,128)}, f32[512,256]{1,0:T(8,128)}) custom-call(bf16[1024,1024]{1,0:T(8,128)(2,1)} %f_hbm.1, bf16[512,1024]{1,0:T(8,128)(2,1)} %c_hbm.1, bf16[1024,256]{1,0:T(8,128)(2,1)} %t_hbm.1), custom_call_target="tpu_custom_call" | custom-call | tf_op jit(solution)/shard_map/pallas_call | solution.py:493
  128.4 1.9 %copy.7 = f32[512,256]{1,0:T(8,128)} copy(f32[512,256]{1,0:T(8,128)} %get-tuple-element.4) | data formatting | bytes 1048576
  130.3 1.9 %copy.8 = f32[512,256]{1,0:T(8,128)} copy(f32[512,256]{1,0:T(8,128)} %get-tuple-element.5) | data formatting | bytes 1048576

commit v5 on v4

--- a/solution.py
+++ b/solution.py
@@ -220,13 +220,15 @@
         dst[zl] = src[seat]
         return jnp.sum(dst[...].astype(F32), axis=0)
 
-    def share_columns(h, step, after):
+    def share_columns(h, step, after, before=lambda: None, meanwhile=lambda: None):
         buf, send, recv = vec.at[h, step], ag_s.at[h, step], ag_r.at[h, step]
         pair_send, pair_recv = sib_s.at[h, step], sib_r.at[h, step]
         mine = buf.at[o]
 
         @pl.when(owning)
         def _():
+            before()
+
             def go(z):
                 copy_to(mine, mine, send, recv.at[seat], line(z)).start()
 
@@ -235,6 +237,7 @@
             after()
 
         yield
+        meanwhile()
 
         def relay(k, z):
             piece = buf.at[c * 4 + k]
@@ -242,7 +245,6 @@
             copy_to(piece, piece, pair_send, pair_recv, sibling).start()
 
         others(4, FIRST, relay)
-        yield
 
         many(buf, 4, pair_send, pair_recv).wait()
         pl.when(owning)(lambda: many(buf, 7, send, recv.at[0]).wait_send())
@@ -337,7 +339,6 @@
         told = str_.at[h, step]
         stats = lambda q: sts.at[h, step, q], told, st_s.at[h, step], st_r.at[h, step]
         tell_owners(*stats)
-        yield
         rems[h, step] = pairs(h, 1 + step).astype(BF16)
         moved = rems.at[h, step], remr.at[h, step], rem_s.at[h, step], rem_r.at[h, step]
         to_owners(*moved)
@@ -360,7 +361,6 @@
         project(h, lambda: tt[h])
         yield
         pair_up(h, 0).start()
-        yield
         both = pairs(h, 0)
         high = both.astype(BF16)
         his[h] = high
@@ -435,21 +435,27 @@
             loop(15, go)
 
         yield from image_of(h, 1, close)
-        yield from share_columns(h, 2, announce)
-
-        sent_or_told(8, lambda count: many(finr.at[h], count, send_all, recv_all).wait_recv())
+        cols = pl.ds(h * 128, 128)
+
+        def finish_coef():
+            sent_or_told(8, lambda count: many(finr.at[h], count, send_all, recv_all).wait_recv())
+            first, second = from_rows(finr[h], 0), from_rows(finr[h], 1)
+            part[h] = first * vec[h, 0].astype(F32) + second * vec[h, 1].astype(F32)
+
+            def turn(k):
+                rows = rows_at(k, 128)
+                coef_ref[rows, cols] = jnp.transpose(part[h, :, :, rows].reshape(128, 128))
+
+            loop(4, turn)
+
+        yield from share_columns(h, 2, lambda: None, announce, finish_coef)
         pl.when(owning)(lambda: many(snr.at[h, 0], 15, send_all, recv_all).wait_send())
 
-        first, second = from_rows(finr[h], 0), from_rows(finr[h], 1)
-        part[h] = first * vec[h, 0].astype(F32) + second * vec[h, 1].astype(F32)
-
-        def turn(k):
+        def turn_residual(k):
             rows = rows_at(k, 128)
-            cols = pl.ds(h * 128, 128)
-            coef_ref[rows, cols] = jnp.transpose(part[h, :, :, rows].reshape(128, 128))
             res_ref[rows, cols] = jnp.transpose(vec[h, 2, :, :, rows].astype(F32).reshape(128, 128))
 
-        loop(4, turn)
+        loop(4, turn_residual)
 
     chains = [chain(0), chain(1)]
     for half in chains:

time: 132 us -> 131 us (level)
  Pallas kernels: 128 us -> 126 us
    pallas_call x1, Pallas kernels: 128 us -> 126 us  [on_device(): pl.pallas_call(functools.partial(kernel, n_total), out_shape=(out, out),...]
where the time goes in v5:
time: 131 us
  Pallas kernels  126 us (96%)
  local copies, waits for them, and re-layouts  3.74 us (3%)
    pallas_call x1, Pallas kernels, on_device(): pl.pallas_call(functools.partial(kernel, n_total), out_shape=(out, out),...  126 us
    unnamed x2, local copies, waits for them, and re-layouts  3.74 us

profile of v5, /device:TPU:1, one launch (start us, length us, event | category | flops | bytes accessed | tf_op | source)
XLA Modules:
  0.0 130.5 jit_solution(17180561518252188599)
XLA Ops:
  0.6 126.2 %shard_map.50 = (f32[512,256]{1,0:T(8,128)}, f32[512,256]{1,0:T(8,128)}) custom-call(bf16[1024,1024]{1,0:T(8,128)(2,1)} %f_hbm.1, bf16[512,1024]{1,0:T(8,128)(2,1)} %c_hbm.1, bf16[1024,256]{1,0:T(8,128)(2,1)} %t_hbm.1), custom_call_target="tpu_custom_call" | custom-call | tf_op jit(solution)/shard_map/pallas_call | solution.py:499
  126.8 1.9 %copy.7 = f32[512,256]{1,0:T(8,128)} copy(f32[512,256]{1,0:T(8,128)} %get-tuple-element.4) | data formatting | bytes 1048576
  128.7 1.9 %copy.8 = f32[512,256]{1,0:T(8,128)} copy(f32[512,256]{1,0:T(8,128)} %get-tuple-element.5) | data formatting | bytes 1048576

commit v6 on v5

--- a/solution.py
+++ b/solution.py
@@ -68,7 +68,7 @@
         body(k)
         return carry
 
-    lax.fori_loop(0, count, step, 0)
+    lax.fori_loop(0, count, step, 0, unroll=count < 6)
 
 
 def kernel(

time: 131 us -> 126 us (0.962)
  Pallas kernels: 126 us -> 122 us
    pallas_call x1, Pallas kernels: 126 us -> 122 us  [on_device(): pl.pallas_call(functools.partial(kernel, n_total), out_shape=(out, out),...]
where the time goes in v6:
time: 126 us
  Pallas kernels  122 us (97%)
  local copies, waits for them, and re-layouts  3.74 us (3%)
    pallas_call x1, Pallas kernels, on_device(): pl.pallas_call(functools.partial(kernel, n_total), out_shape=(out, out),...  122 us
    unnamed x2, local copies, waits for them, and re-layouts  3.74 us

profile of v6, /device:TPU:1, one launch (start us, length us, event | category | flops | bytes accessed | tf_op | source)
XLA Modules:
  0.0 126.1 jit_solution(13736870110087024466)
XLA Ops:
  0.6 121.7 %shard_map.50 = (f32[512,256]{1,0:T(8,128)}, f32[512,256]{1,0:T(8,128)}) custom-call(bf16[1024,1024]{1,0:T(8,128)(2,1)} %f_hbm.1, bf16[512,1024]{1,0:T(8,128)(2,1)} %c_hbm.1, bf16[1024,256]{1,0:T(8,128)(2,1)} %t_hbm.1), custom_call_target="tpu_custom_call" | custom-call | tf_op jit(solution)/shard_map/pallas_call | solution.py:499
  122.3 1.9 %copy.7 = f32[512,256]{1,0:T(8,128)} copy(f32[512,256]{1,0:T(8,128)} %get-tuple-element.4) | data formatting | bytes 1048576
  124.2 1.9 %copy.8 = f32[512,256]{1,0:T(8,128)} copy(f32[512,256]{1,0:T(8,128)} %get-tuple-element.5) | data formatting | bytes 1048576
